TPU v7x, 32 devices: a whole 2x2x4 slice. The times are simulated.
32 devices in a mesh: cp: 4 (over y, x), grp: 8 (over z, core).
Axes of the slice: x: 2, y: 2, z: 4, core: 2. Of those that a mesh axis runs over, the one named last changes fastest.
Arguments:
- queries: bfloat16 [16, 512, 2048], P('grp', 'cp'), may hold values from -108 to 108
- keys: bfloat16 [16, 512, 2048], P('grp', 'cp'), may hold values from -4 to 4
- values: bfloat16 [16, 512, 2048], P('grp', 'cp'), may hold values from -6 to 6
- lengths: int32 [16], P('grp'), may hold values from 128 to 512
- frame_map: bfloat16 [2048, 2176], replicated, may hold values from -0.125 to 0.125
- proj_weight: bfloat16 [2176, 4096], P('grp', 'cp'), may hold values from -0.125 to 0.125
- head_weight: bfloat16 [4096, 256], P('cp'), may hold values from -0.375 to 0.375
- act_embed: float32 [7, 4096], P(None, 'cp'), may hold values from -0.5 to 0.5
- actions: int32 [16, 7], P('grp'), may hold values from 0 to 255
- action_mask: int32 [16, 7], P('grp'), may hold values 0 or 1
- group_ids: int32 [16], P('grp'), may hold values from 0 to 1
- rewards: float32 [16], P('grp'), may hold values from -6 to 6
Outputs:
- logprobs: float32 [16, 7], P('grp')
- grad_proj: bfloat16 [2176, 4096], P('grp', 'cp')
- grad_head: bfloat16 [4096, 256], P('cp')
All inputs are finite; a program needn't handle non-finite values. No bound on the sum of `action_mask` on one device may be relied on, other than what follows from the above.
Results may differ from a plain program's by a relative error of at most 0.018.
Values may be sent and summed in bfloat16 or wider, within the bound.
A program may use at most 128 MiB of HBM per device.

v0:
```python
import math
import jax
import jax.numpy as jnp
from jax import lax
from jax.sharding import PartitionSpec as P

HD = 128
SQRT_HALF = 0.7071067811865476
INV_ROOT_TAU = 0.3989422804014327
NEG_LARGE = -1e30


def gelu_exact(values_in):
    return 0.5 * values_in * (1.0 + lax.erf(values_in * SQRT_HALF))


def gelu_slope(values_in):
    return (
        0.5 * (1.0 + lax.erf(values_in * SQRT_HALF))
        + values_in * jnp.exp(-0.5 * values_in * values_in) * INV_ROOT_TAU
    )


def fetch_columns(proj_weight):
    return lax.all_gather(proj_weight, "grp", axis=0, tiled=True)


def attention(queries, keys, values, lengths):
    episodes_here, tokens_here, att_width = queries.shape
    head_count = att_width // HD
    query_heads = queries.reshape(episodes_here, tokens_here, head_count, HD)
    key_heads = keys.reshape(episodes_here, tokens_here, head_count, HD)
    value_heads = values.reshape(episodes_here, tokens_here, head_count, HD)
    query_all, key_all, value_all = (
        lax.all_to_all(query_heads, "cp", split_axis=2, concat_axis=1, tiled=True),
        lax.all_to_all(key_heads, "cp", split_axis=2, concat_axis=1, tiled=True),
        lax.all_to_all(value_heads, "cp", split_axis=2, concat_axis=1, tiled=True),
    )
    seq_span = query_all.shape[1]
    scores = jnp.einsum(
        "eihd,ejhd->ehij", query_all, key_all, preferred_element_type=jnp.float32
    ) / math.sqrt(HD)
    live_keys = (jnp.arange(seq_span, dtype=jnp.int32)[None, :] < lengths[:, None])[
        :, None, None, :
    ]
    scores = jnp.where(live_keys, scores, NEG_LARGE)
    row_max = jnp.max(scores, axis=-1, keepdims=True)
    probs = jnp.where(live_keys, jnp.exp(scores - row_max), 0.0)
    row_total = jnp.sum(probs, axis=-1)
    weighted = jnp.einsum(
        "ehij,ejhd->eihd", probs.astype(jnp.bfloat16), value_all, preferred_element_type=jnp.float32
    )
    output = (weighted / jnp.transpose(row_total, (0, 2, 1))[..., None]).astype(jnp.bfloat16)
    returned = lax.all_to_all(output, "cp", split_axis=1, concat_axis=2, tiled=True)
    return returned.reshape(episodes_here, tokens_here, att_width)


def per_device(
    queries,
    keys,
    values,
    lengths,
    frame_map,
    proj_weight,
    head_weight,
    act_embed,
    actions,
    action_mask,
    group_ids,
    rewards,
):
    episodes_here, tokens_here, att_width = queries.shape
    action_count = act_embed.shape[0]
    lengths_real = lengths.astype(jnp.float32)
    attended = attention(queries, keys, values, lengths)
    proj_cols = fetch_columns(proj_weight)
    frames = jnp.dot(
        attended.reshape(episodes_here * tokens_here, att_width),
        frame_map,
        preferred_element_type=jnp.float32,
    )
    frames = frames.astype(jnp.bfloat16).reshape(episodes_here, tokens_here, frame_map.shape[1])
    all_frames = lax.all_gather(frames, "cp", axis=1, tiled=True)
    seq_span = all_frames.shape[1]
    flat_frames = all_frames.reshape(episodes_here * seq_span, all_frames.shape[2])
    col_count = proj_cols.shape[1]
    pre_act = jnp.dot(flat_frames, proj_cols, preferred_element_type=jnp.float32).reshape(
        episodes_here, seq_span, col_count
    )
    hidden = gelu_exact(pre_act)
    token_mask = (jnp.arange(seq_span, dtype=jnp.int32)[None, :] < lengths[:, None]).astype(
        jnp.float32
    )
    pooled = jnp.sum(token_mask[:, :, None] * hidden, axis=1) / lengths_real[:, None]
    sum_input = pooled[:, None, :] + act_embed[None, :, :]
    head_input = sum_input.astype(jnp.bfloat16).reshape(episodes_here * action_count, col_count)
    partial_logits = jnp.dot(head_input, head_weight, preferred_element_type=jnp.float32)
    episodes_total = episodes_here * lax.axis_size("grp")
    group_count = max(1, episodes_total // 8)
    membership = (group_ids[:, None] == jnp.arange(group_count, dtype=jnp.int32)[None, :]).astype(
        jnp.float32
    )
    masked = action_mask.astype(jnp.float32)
    logits = lax.psum(partial_logits, "cp")
    reward_sums, squares, group_sizes, mask_total = lax.psum(
        (
            jnp.sum(membership * rewards[:, None], axis=0),
            jnp.sum(membership * (rewards * rewards)[:, None], axis=0),
            jnp.sum(membership, axis=0),
            jnp.sum(masked),
        ),
        "grp",
    )
    log_all = jax.nn.log_softmax(logits, axis=-1)
    bin_ids = jnp.arange(head_weight.shape[1], dtype=jnp.int32)
    picked = (actions.reshape(-1)[:, None] == bin_ids[None, :]).astype(jnp.float32)
    logprobs = jnp.sum(picked * log_all, axis=-1).reshape(episodes_here, action_count)
    size_floor = jnp.maximum(group_sizes, 1.0)
    group_mean = reward_sums / size_floor
    variance = squares / size_floor - group_mean * group_mean
    group_scale = jnp.sqrt(jnp.maximum(variance, 1.0))
    advantage = (rewards - jnp.sum(membership * group_mean[None, :], axis=1)) / jnp.sum(
        membership * group_scale[None, :], axis=1
    )
    loss_weight = (-masked * advantage[:, None] / jnp.maximum(mask_total, 1.0)).reshape(-1)
    logit_grad = (loss_weight[:, None] * (picked - jnp.exp(log_all))).astype(jnp.bfloat16)
    head_term = lax.dot_general(
        head_input, logit_grad, (((0,), (0,)), ((), ())), preferred_element_type=jnp.float32
    )
    grad_head = lax.psum(head_term.astype(jnp.bfloat16), "grp")
    pull_back = lax.dot_general(
        logit_grad, head_weight, (((1,), (1,)), ((), ())), preferred_element_type=jnp.float32
    )
    pool_grad = jnp.sum(pull_back.reshape(episodes_here, action_count, col_count), axis=1)
    scaled_mask = token_mask / lengths_real[:, None]
    act_grad = (scaled_mask[:, :, None] * pool_grad[:, None, :] * gelu_slope(pre_act)).astype(
        jnp.bfloat16
    )
    act_flat = act_grad.reshape(episodes_here * seq_span, col_count)
    grad_proj = lax.psum_scatter(
        lax.dot_general(
            flat_frames, act_flat, (((0,), (0,)), ((), ())), preferred_element_type=jnp.float32
        ).astype(jnp.bfloat16),
        "grp",
        scatter_dimension=0,
        tiled=True,
    )
    return (logprobs, grad_proj, grad_head)


def solution(mesh):
    in_specs = (
        P("grp", "cp", None),
        P("grp", "cp", None),
        P("grp", "cp", None),
        P("grp"),
        P(),
        P("grp", "cp"),
        P("cp", None),
        P(None, "cp"),
        P("grp", None),
        P("grp", None),
        P("grp"),
        P("grp"),
    )
    out_specs = (P("grp", None), P("grp", "cp"), P("cp", None))
    return jax.shard_map(
        per_device, mesh=mesh, in_specs=in_specs, out_specs=out_specs, check_vma=False
    )
```

profile of v0, /device:TPU:0, one launch (start us, length us, event | category | flops | bytes accessed | tf_op | source)
XLA Modules:
  0.0 302.5 jit_solution(11430559681268954911)
XLA Ops:
  7.9 1.6 copy.51
  10.6 5.2 %all-to-all-start = ((bf16[2,128,16,128]{1,3,0,2:T(8,128)(2,1)}), bf16[2,128,16,128]{1,3,0,2:T(8,128)(2,1)S(1)}, u32[]{:S(2)}, u32[]{:S(2)}) async-start(bf16[2,128,16,128]{1,3,0,2:T(8,128)(2,1)} %copy.52), calls=%async_computation | async-start | bytes 2097152 | tf_op jit(solution)/shard_map/all_to_all | solution.py:35
  15.8 1.6 copy.55
  18.5 10.9 %all-to-all-done = bf16[2,128,16,128]{1,3,0,2:T(8,128)(2,1)S(1)} async-done(((bf16[2,128,16,128]{1,3,0,2:T(8,128)(2,1)}), bf16[2,128,16,128]{1,3,0,2:T(8,128)(2,1)S(1)}, u32[]{:S(2)}, u32[]{:S(2)}) %all-to-all-start) | async-done | bytes 1048608 | tf_op jit(solution)/shard_map/all_to_all | solution.py:35
  29.4 3.5 %all-to-all-start.1 = ((bf16[2,128,16,128]{1,3,0,2:T(8,128)(2,1)}), bf16[2,128,16,128]{1,3,0,2:T(8,128)(2,1)S(1)}, u32[]{:S(2)}, u32[]{:S(2)}) async-start(bf16[2,128,16,128]{1,3,0,2:T(8,128)(2,1)} %copy.56), calls=%async_computation.1 | async-start | bytes 2097152 | tf_op jit(solution)/shard_map/all_to_all | solution.py:36
  32.9 2.3 copy.59
  35.2 2.3 copy.60
  37.5 8.6 %all-to-all-done.1 = bf16[2,128,16,128]{1,3,0,2:T(8,128)(2,1)S(1)} async-done(((bf16[2,128,16,128]{1,3,0,2:T(8,128)(2,1)}), bf16[2,128,16,128]{1,3,0,2:T(8,128)(2,1)S(1)}, u32[]{:S(2)}, u32[]{:S(2)}) %all-to-all-start.1) | async-done | bytes 1048608 | tf_op jit(solution)/shard_map/all_to_all | solution.py:36
  46.2 4.3 %all-to-all-start.2 = ((bf16[2,128,16,128]{1,3,0,2:T(8,128)(2,1)}), bf16[2,128,16,128]{1,3,0,2:T(8,128)(2,1)}, u32[]{:S(2)}, u32[]{:S(2)}) async-start(bf16[2,128,16,128]{1,3,0,2:T(8,128)(2,1)} %copy.60), calls=%async_computation.2 | async-start | bytes 2097152 | tf_op jit(solution)/shard_map/all_to_all | solution.py:37
  51.9 1.4 copy.58
  53.2 10.5 %all-to-all-done.2 = bf16[2,128,16,128]{1,3,0,2:T(8,128)(2,1)} async-done(((bf16[2,128,16,128]{1,3,0,2:T(8,128)(2,1)}), bf16[2,128,16,128]{1,3,0,2:T(8,128)(2,1)}, u32[]{:S(2)}, u32[]{:S(2)}) %all-to-all-start.2) | async-done | bytes 1048608 | tf_op jit(solution)/shard_map/all_to_all | solution.py:37
  63.7 1.6 copy.62
  65.4 6.8 %fusion.33 = (f32[2,4,512]{2,1,0:T(4,128)S(1)}, bf16[2,4,512,512]{2,3,1,0:T(8,128)(2,1)}) fusion(pred[2,512]{1,0:T(4,128)(4,1)S(1)} %get-tuple-element.15, bf16[2,512,4,128]{3,1,2,0:T(8,128)(2,1)S(1)} %bitcast.54, bf16[2,512,4,128]{3,1,2,0:T(8,128)(2,1)} %bitcast.55), kind=kOutput, calls=%fused_computation.58 | convolution fusion | flops 549454336 | bytes 6308864 | tf_op jit(solution)/shard_map/sub | solution.py:48
  72.2 3.9 %fusion.16 = bf16[2,512,4,128]{3,1,2,0:T(8,128)(2,1)S(1)} fusion(bf16[2,512,4,128]{3,1,2,0:T(8,128)(2,1)S(1)} %bitcast.56, bf16[2,4,512,512]{2,3,1,0:T(8,128)(2,1)} %get-tuple-element.17, f32[2,512,4]{1,2,0:T(4,128)S(1)} %bitcast.57), kind=kOutput, calls=%fused_computation.23 | convolution fusion | flops 537919488 | bytes 6307840 | tf_op jit(solution)/shard_map/ehij,ejhd->eihd/dot_general | solution.py:50
  76.9 16.1 %all_to_all.69 = bf16[2,512,4,128]{3,2,0,1:T(4,128)(2,1)S(1)} all-to-all(bf16[2,512,4,128]{3,2,0,1:T(4,128)(2,1)S(1)} %copy.64), channel_id=1, replica_groups=mesh['cp'=4,'grp'=8] {'cp'}, dimensions={1} | all-to-all | bytes 2097152 | tf_op jit(solution)/shard_map/all_to_all | solution.py:54
  94.3 7.2 %convolution_convert_fusion = bf16[256,2176]{1,0:T(8,128)(2,1)} fusion(bf16[256,2048]{1,0:T(8,128)(2,1)S(1)} %reshape_reshape.3, bf16[2048,2176]{1,0:T(8,128)(2,1)} %param.16), kind=kOutput, calls=%fused_computation.21 | convolution fusion | flops 2282258432 | bytes 11075584 | tf_op jit(solution)/shard_map/dot_general | solution.py:77
  102.3 15.2 %all-reduce = (f32[]{:T(128)}, f32[2]{0:T(128)S(1)}, f32[2]{0:T(128)S(1)}, f32[2]{0:T(128)S(1)}) all-reduce(f32[]{:T(128)} %convert_reduce_fusion.1, f32[2]{0:T(128)S(1)} %get-tuple-element.7, f32[2]{0:T(128)S(1)} %get-tuple-element.6, f32[2]{0:T(128)S(1)} %get-tuple-element.5), channel_id=1, replica_groups=mesh['cp'=4,'grp'=8] {'grp'}, use_global_device_ids=true, to_apply=%region_16.17 | all-reduce | flops 7 | bytes 56 | tf_op jit(solution)/shard_map/psum | solution.py:105
  118.7 37.5 %all-gather.3.cloned.1.call-done = bf16[2,512,2176]{2,1,0:T(8,128)(2,1)} async-done(((bf16[2,128,2176]{2,1,0:T(8,128)(2,1)}), bf16[2,512,2176]{2,1,0:T(8,128)(2,1)}) %all-gather.3.cloned.1.call-update) | async-done | bytes 4456464 | tf_op jit(solution)/shard_map/all_gather | solution.py:83
  156.2 9.9 %multiply_reduce_fusion = (f32[2,1024]{1,0:T(2,128)S(1)}, f32[2,512,1024]{2,1,0:T(8,128)}) fusion(f32[2,512]{1,0:T(2,128)S(1)} %get-tuple-element.14, bf16[2,512,2176]{2,1,0:T(8,128)(2,1)} %all-gather.3.cloned.1.call-done, bf16[2176,1024]{1,0:T(8,128)(2,1)} %all-gather.5.cloned.1.call-done), kind=kOutput, calls=%fused_computation.14 | convolution fusion | flops 4569692160 | bytes 13119488 | tf_op jit(solution)/shard_map/dot_general | solution.py:87
  166.4 15.1 %psum.42 = f32[14,256]{1,0:T(8,128)S(1)} all-reduce(f32[14,256]{1,0:T(8,128)S(1)} %fusion.34), channel_id=1, replica_groups=mesh['cp'=4,'grp'=8] {'cp'}, use_global_device_ids=true, to_apply=%region_3.4 | all-reduce | flops 3584 | bytes 28672 | tf_op jit(solution)/shard_map/psum | solution.py:104
  183.4 10.3 %bitcast_convert_fusion = bf16[2176,1024]{1,0:T(8,128)(2,1)} fusion(bf16[2,512,2176]{2,1,0:T(8,128)(2,1)} %all-gather.3.cloned.1.call-done, f32[2,512,1024]{2,1,0:T(8,128)} %get-tuple-element.19, f32[2,1024]{1,0:T(2,128)S(1)} %reduce_sum.110, f32[2,512]{1,0:T(2,128)S(1)} %broadcast_divide_fusion.1), kind=kOutput, calls=%fused_computation.1 | convolution fusion | flops 4577165312 | bytes 13119488 | tf_op jit(solution)/shard_map/dot_general | solution.py:141
  194.5 45.4 %all-reduce.3.cloned.1.call-done = bf16[1024,256]{1,0:T(8,128)(2,1)} async-done(((bf16[1024,256]{1,0:T(8,128)(2,1)}), bf16[1024,256]{1,0:T(8,128)(2,1)}) %all-reduce.3.cloned.1.call-update) | async-done | bytes 524304 | tf_op jit(solution)/shard_map/psum | solution.py:130
  239.9 54.2 %reduce-scatter.2.cloned.1.call-done = bf16[272,1024]{1,0:T(8,128)(2,1)} async-done(((bf16[2176,1024]{1,0:T(8,128)(2,1)}), bf16[272,1024]{1,0:T(8,128)(2,1)}) %reduce-scatter.2.cloned.1.call-update) | async-done | bytes 557072 | tf_op jit(solution)/shard_map/reduce_scatter | solution.py:140
  294.1 1.9 copy.75
  (56 shorter events, 10.5 us)
Async XLA Ops:
  7.2 159.1 %copy-start = (bf16[1024,256]{1,0:T(8,128)(2,1)S(1)}, bf16[1024,256]{1,0:T(8,128)(2,1)}, u32[]{:S(2)}) copy-start(bf16[1024,256]{1,0:T(8,128)(2,1)} %param.18) | copy-start | bytes 1572868
  7.2 111.5 %all-gather.5.cloned.1.call-start = ((), (), s32[]{:S(2)}) async-start(), calls=%async_computation.6 | async-start | bytes 5013504 | tf_op jit(solution)/shard_map/all_gather | solution.py:25
  10.6 18.8 %all-to-all-start = ((bf16[2,128,16,128]{1,3,0,2:T(8,128)(2,1)}), bf16[2,128,16,128]{1,3,0,2:T(8,128)(2,1)S(1)}, u32[]{:S(2)}, u32[]{:S(2)}) async-start(bf16[2,128,16,128]{1,3,0,2:T(8,128)(2,1)} %copy.52), calls=%async_computation | async-start | bytes 2097152 | tf_op jit(solution)/shard_map/all_to_all | solution.py:35
  18.5 32.0 %copy-start.5 = (s32[2]{0:T(128)S(1)}, s32[2]{0:T(128)}, u32[]{:S(2)}) copy-start(s32[2]{0:T(128)} %param.15) | copy-start | bytes 28
  29.4 16.8 %all-to-all-start.1 = ((bf16[2,128,16,128]{1,3,0,2:T(8,128)(2,1)}), bf16[2,128,16,128]{1,3,0,2:T(8,128)(2,1)S(1)}, u32[]{:S(2)}, u32[]{:S(2)}) async-start(bf16[2,128,16,128]{1,3,0,2:T(8,128)(2,1)} %copy.56), calls=%async_computation.1 | async-start | bytes 2097152 | tf_op jit(solution)/shard_map/all_to_all | solution.py:36
  46.2 17.6 %all-to-all-start.2 = ((bf16[2,128,16,128]{1,3,0,2:T(8,128)(2,1)}), bf16[2,128,16,128]{1,3,0,2:T(8,128)(2,1)}, u32[]{:S(2)}, u32[]{:S(2)}) async-start(bf16[2,128,16,128]{1,3,0,2:T(8,128)(2,1)} %copy.60), calls=%async_computation.2 | async-start | bytes 2097152 | tf_op jit(solution)/shard_map/all_to_all | solution.py:37
  50.4 105.8 %all-gather.3.cloned.1.call-start = ((), (), s32[]{:S(2)}) async-start(), calls=%async_computation.5 | async-start | bytes 5570560 | tf_op jit(solution)/shard_map/all_gather | solution.py:83
  51.9 13.5 %copy-start.1 = (bf16[2,4,128,4,128]{4,2,1,3,0:T(8,128)(2,1)S(1)}, bf16[2,4,128,4,128]{4,2,1,3,0:T(8,128)(2,1)}, u32[]{:S(2)}) copy-start(bf16[2,4,128,4,128]{4,2,1,3,0:T(8,128)(2,1)} %copy.54) | copy-start | bytes 3145732
  94.2 7.3 %copy-start.4 = (f32[2]{0:T(128)S(1)}, f32[2]{0:T(128)}, u32[]{:S(2)}) copy-start(f32[2]{0:T(128)} %param.23) | copy-start | bytes 28
  94.2 7.4 %copy-start.6 = (s32[2,7]{1,0:T(2,128)S(1)}, s32[2,7]{1,0:T(2,128)}, u32[]{:S(2)}) copy-start(s32[2,7]{1,0:T(2,128)} %param.21) | copy-start | bytes 172
  94.2 8.0 %copy-start.3 = (s32[2]{0:T(128)S(1)}, s32[2]{0:T(128)}, u32[]{:S(2)}) copy-start(s32[2]{0:T(128)} %param.22) | copy-start | bytes 28
  94.3 23.3 %copy-start.7 = (s32[2,7]{1,0:T(2,128)S(1)}, s32[2,7]{1,0:T(2,128)}, u32[]{:S(2)}) copy-start(s32[2,7]{1,0:T(2,128)} %param.20) | copy-start | bytes 172
  101.5 138.4 %all-reduce.3.cloned.1.call-start = ((), (), s32[]{:S(2)}) async-start(), calls=%async_computation.8 | async-start | bytes 1048576 | tf_op jit(solution)/shard_map/psum | solution.py:130
  156.2 10.0 %copy-start.2 = (f32[7,1024]{1,0:T(8,128)S(1)}, f32[7,1024]{1,0:T(8,128)}, u32[]{:S(2)}) copy-start(f32[7,1024]{1,0:T(8,128)} %param.19) | copy-start | bytes 86020
  183.3 110.8 %reduce-scatter.2.cloned.1.call-start = ((), (), s32[]{:S(2)}) async-start(), calls=%async_computation.7 | async-start | bytes 5013504 | tf_op jit(solution)/shard_map/reduce_scatter | solution.py:140
Sparse Core Ops, SparseCore 0:
  9.6 51.7 all-gather.4
  101.6 54.4 all-gather.2
  183.4 56.4 all-reduce.2
  242.7 51.4 reduce-scatter.1
where the time goes:
time: 303 us
  waiting for transfers between devices  168 us (55%)
  blocking collectives  46.4 us (15%)
  matrix products  39.8 us (13%)
  local copies, waits for them, and re-layouts  19 us (6%)
  between operations  14.6 us (5%)
  starting transfers between devices  13.1 us (4%)
    reduce_scatter x1, waiting for transfers between devices, per_device(): lax.psum_scatter(lax.dot_general(flat_frames, act_flat, (((0,), (0,)), ((...  54.2 us
    psum x1, waiting for transfers between devices, per_device(): grad_head = lax.psum(head_term.astype(jnp.bfloat16), 'grp')  45.4 us
    all_gather x1, waiting for transfers between devices, per_device(): all_frames = lax.all_gather(frames, 'cp', axis=1, tiled=True)  37.5 us
    all_to_all x1, blocking collectives, attention(): lax.all_to_all(output, 'cp', split_axis=1, concat_axis=2, tiled=True)  16.1 us
    psum x1, blocking collectives, per_device(): lax.psum((jnp.sum(membership * rewards[:, None], axis=0), jnp.sum(members...  15.2 us
    psum x1, blocking collectives, per_device(): logits = lax.psum(partial_logits, 'cp')  15.1 us
    all_to_all x1, waiting for transfers between devices, attention(): lax.all_to_all(query_heads, 'cp', split_axis=2, concat_axis=1, tiled=True)  10.9 us
    all_to_all x1, waiting for transfers between devices, attention(): lax.all_to_all(value_heads, 'cp', split_axis=2, concat_axis=1, tiled=True)  10.5 us
  transfers between devices with their start and end apart: 7, of which 6 were waited for; matrix products, arithmetic and copies ran while one was open for 15% of the time, Pallas kernels for 0%

commit v1 on v0

--- a/solution.py
+++ b/solution.py
@@ -80,7 +80,7 @@
         preferred_element_type=jnp.float32,
     )
     frames = frames.astype(jnp.bfloat16).reshape(episodes_here, tokens_here, frame_map.shape[1])
-    all_frames = lax.all_gather(frames, "cp", axis=1, tiled=True)
+    all_frames = jnp.concatenate(lax.all_gather(frames, "cp"), axis=1)
     seq_span = all_frames.shape[1]
     flat_frames = all_frames.reshape(episodes_here * seq_span, all_frames.shape[2])
     col_count = proj_cols.shape[1]

time: 303 us -> 303 us (level)
  other arithmetic: 1.73 us -> 5.74 us
    convert_element_type x0 -> x1, other arithmetic: none -> 4.01 us  [per_device(): (scaled_mask[:, :, None] * pool_grad[:, None, :] * gelu_slope(pre_act)).a...]
  transfers between devices with their start and end apart: 7 -> 7, of which waited for: 6 -> 6; matrix products, arithmetic and copies ran while one was open for 15% -> 16% of each run, Pallas kernels for 0% -> 0%
where the time goes in v1:
time: 303 us
  waiting for transfers between devices  165 us (54%)
  blocking collectives  46.4 us (15%)
  matrix products  38.4 us (13%)
  local copies, waits for them, and re-layouts  19 us (6%)
  between operations  14.6 us (5%)
  starting transfers between devices  13.1 us (4%)
  other arithmetic  5.74 us (2%)
    reduce_scatter x1, waiting for transfers between devices, per_device(): lax.psum_scatter(lax.dot_general(flat_frames, act_flat, (((0,), (0,)), ((...  54.2 us
    psum x1, waiting for transfers between devices, per_device(): grad_head = lax.psum(head_term.astype(jnp.bfloat16), 'grp')  42.9 us
    all_gather x1, waiting for transfers between devices, per_device(): all_frames = jnp.concatenate(lax.all_gather(frames, 'cp'), axis=1)  37.5 us
    all_to_all x1, blocking collectives, attention(): lax.all_to_all(output, 'cp', split_axis=1, concat_axis=2, tiled=True)  16.1 us
    psum x1, blocking collectives, per_device(): lax.psum((jnp.sum(membership * rewards[:, None], axis=0), jnp.sum(members...  15.2 us
    psum x1, blocking collectives, per_device(): logits = lax.psum(partial_logits, 'cp')  15.1 us
    all_to_all x1, waiting for transfers between devices, attention(): lax.all_to_all(value_heads, 'cp', split_axis=2, concat_axis=1, tiled=True)  11 us
    all_to_all x1, waiting for transfers between devices, attention(): lax.all_to_all(key_heads, 'cp', split_axis=2, concat_axis=1, tiled=True)  10.5 us
  transfers between devices with their start and end apart: 7, of which 6 were waited for; matrix products, arithmetic and copies ran while one was open for 16% of the time, Pallas kernels for 0%

profile of v1, /device:TPU:0, one launch (start us, length us, event | category | flops | bytes accessed | tf_op | source)
XLA Modules:
  0.0 302.6 jit_solution(17193684282912918958)
XLA Ops:
  7.9 1.6 copy.59
  10.6 5.2 %all-to-all-start.2 = ((bf16[2,128,16,128]{1,3,0,2:T(8,128)(2,1)}), bf16[2,128,16,128]{1,3,0,2:T(8,128)(2,1)S(1)}, u32[]{:S(2)}, u32[]{:S(2)}) async-start(bf16[2,128,16,128]{1,3,0,2:T(8,128)(2,1)} %copy.60), calls=%async_computation.2 | async-start | bytes 2097152 | tf_op jit(solution)/shard_map/all_to_all | solution.py:37
  15.8 1.6 copy.51
  18.5 11.0 %all-to-all-done.2 = bf16[2,128,16,128]{1,3,0,2:T(8,128)(2,1)S(1)} async-done(((bf16[2,128,16,128]{1,3,0,2:T(8,128)(2,1)}), bf16[2,128,16,128]{1,3,0,2:T(8,128)(2,1)S(1)}, u32[]{:S(2)}, u32[]{:S(2)}) %all-to-all-start.2) | async-done | bytes 1048608 | tf_op jit(solution)/shard_map/all_to_all | solution.py:37
  29.4 3.5 %all-to-all-start = ((bf16[2,128,16,128]{1,3,0,2:T(8,128)(2,1)}), bf16[2,128,16,128]{1,3,0,2:T(8,128)(2,1)S(1)}, u32[]{:S(2)}, u32[]{:S(2)}) async-start(bf16[2,128,16,128]{1,3,0,2:T(8,128)(2,1)} %copy.52), calls=%async_computation | async-start | bytes 2097152 | tf_op jit(solution)/shard_map/all_to_all | solution.py:35
  33.0 2.3 copy.55
  35.2 2.3 copy.56
  37.6 8.6 %all-to-all-done = bf16[2,128,16,128]{1,3,0,2:T(8,128)(2,1)S(1)} async-done(((bf16[2,128,16,128]{1,3,0,2:T(8,128)(2,1)}), bf16[2,128,16,128]{1,3,0,2:T(8,128)(2,1)S(1)}, u32[]{:S(2)}, u32[]{:S(2)}) %all-to-all-start) | async-done | bytes 1048608 | tf_op jit(solution)/shard_map/all_to_all | solution.py:35
  46.2 4.2 %all-to-all-start.1 = ((bf16[2,128,16,128]{1,3,0,2:T(8,128)(2,1)}), bf16[2,128,16,128]{1,3,0,2:T(8,128)(2,1)}, u32[]{:S(2)}, u32[]{:S(2)}) async-start(bf16[2,128,16,128]{1,3,0,2:T(8,128)(2,1)} %copy.56), calls=%async_computation.1 | async-start | bytes 2097152 | tf_op jit(solution)/shard_map/all_to_all | solution.py:36
  53.2 10.5 %all-to-all-done.1 = bf16[2,128,16,128]{1,3,0,2:T(8,128)(2,1)} async-done(((bf16[2,128,16,128]{1,3,0,2:T(8,128)(2,1)}), bf16[2,128,16,128]{1,3,0,2:T(8,128)(2,1)}, u32[]{:S(2)}, u32[]{:S(2)}) %all-to-all-start.1) | async-done | bytes 1048608 | tf_op jit(solution)/shard_map/all_to_all | solution.py:36
  63.8 1.6 copy.58
  65.4 6.9 %fusion.24 = (f32[2,4,512]{2,1,0:T(4,128)S(1)}, bf16[2,4,512,512]{2,3,1,0:T(8,128)(2,1)}) fusion(pred[2,512]{1,0:T(4,128)(4,1)S(1)} %get-tuple-element.15, bf16[2,512,4,128]{3,1,2,0:T(8,128)(2,1)} %bitcast.63, bf16[2,512,4,128]{3,1,2,0:T(8,128)(2,1)S(1)} %bitcast.64), kind=kOutput, calls=%fused_computation.50 | convolution fusion | flops 549454336 | bytes 6308864 | tf_op jit(solution)/shard_map/sub | solution.py:48
  72.3 3.9 %fusion.15 = bf16[2,512,4,128]{3,1,2,0:T(8,128)(2,1)S(1)} fusion(bf16[2,512,4,128]{3,1,2,0:T(8,128)(2,1)S(1)} %bitcast.62, bf16[2,4,512,512]{2,3,1,0:T(8,128)(2,1)} %get-tuple-element.17, f32[2,512,4]{1,2,0:T(4,128)S(1)} %bitcast.67), kind=kOutput, calls=%fused_computation.23 | convolution fusion | flops 537919488 | bytes 6307840 | tf_op jit(solution)/shard_map/ehij,ejhd->eihd/dot_general | solution.py:50
  77.0 16.1 %all_to_all.69 = bf16[2,512,4,128]{3,2,0,1:T(4,128)(2,1)S(1)} all-to-all(bf16[2,512,4,128]{3,2,0,1:T(4,128)(2,1)S(1)} %copy.64), channel_id=1, replica_groups=mesh['cp'=4,'grp'=8] {'cp'}, dimensions={1} | all-to-all | bytes 2097152 | tf_op jit(solution)/shard_map/all_to_all | solution.py:54
  94.4 7.2 %convolution_convert_fusion.1 = bf16[256,2176]{1,0:T(8,128)(2,1)} fusion(bf16[256,2048]{1,0:T(8,128)(2,1)S(1)} %reshape_reshape.6, bf16[2048,2176]{1,0:T(8,128)(2,1)} %param.16), kind=kOutput, calls=%fused_computation.21 | convolution fusion | flops 2282258432 | bytes 11075584 | tf_op jit(solution)/shard_map/dot_general | solution.py:77
  102.4 15.2 %all-reduce = (f32[]{:T(128)}, f32[2]{0:T(128)S(1)}, f32[2]{0:T(128)S(1)}, f32[2]{0:T(128)S(1)}) all-reduce(f32[]{:T(128)} %convert_reduce_fusion.1, f32[2]{0:T(128)S(1)} %get-tuple-element.7, f32[2]{0:T(128)S(1)} %get-tuple-element.6, f32[2]{0:T(128)S(1)} %get-tuple-element.5), channel_id=1, replica_groups=mesh['cp'=4,'grp'=8] {'grp'}, use_global_device_ids=true, to_apply=%region_16.17 | all-reduce | flops 7 | bytes 56 | tf_op jit(solution)/shard_map/psum | solution.py:105
  118.8 37.5 %all-gather.3.cloned.1.call-done = bf16[4,2,128,2176]{3,2,0,1:T(8,128)(2,1)} async-done(((bf16[1,2,128,2176]{3,2,0,1:T(8,128)(2,1)}), bf16[4,2,128,2176]{3,2,0,1:T(8,128)(2,1)}) %all-gather.3.cloned.1.call-update) | async-done | bytes 4456464 | tf_op jit(solution)/shard_map/all_gather | solution.py:83
  156.3 9.9 %multiply_reduce_fusion = (f32[2,1024]{1,0:T(2,128)S(1)}, f32[2,512,1024]{2,1,0:T(8,128)}) fusion(f32[2,512]{1,0:T(2,128)S(1)} %get-tuple-element.14, bf16[2,512,2176]{2,1,0:T(8,128)(2,1)} %bitcast.65, bf16[2176,1024]{1,0:T(8,128)(2,1)} %all-gather.5.cloned.1.call-done), kind=kOutput, calls=%fused_computation.14 | convolution fusion | flops 4569692160 | bytes 13119488 | tf_op jit(solution)/shard_map/dot_general | solution.py:87
  166.5 15.1 %psum.42 = f32[14,256]{1,0:T(8,128)S(1)} all-reduce(f32[14,256]{1,0:T(8,128)S(1)} %fusion.25), channel_id=1, replica_groups=mesh['cp'=4,'grp'=8] {'cp'}, use_global_device_ids=true, to_apply=%region_3.4 | all-reduce | flops 3584 | bytes 28672 | tf_op jit(solution)/shard_map/psum | solution.py:104
  183.5 4.0 %fusion.9 = bf16[2,512,1024]{2,1,0:T(8,128)(2,1)S(1)} fusion(f32[2,512,1024]{2,1,0:T(8,128)} %get-tuple-element.19, f32[2,1024]{1,0:T(2,128)S(1)} %reduce_sum.110, f32[2,512]{1,0:T(2,128)S(1)} %broadcast_divide_fusion.1), kind=kLoop, calls=%fused_computation.13 | loop fusion | flops 11534336 | bytes 6303744 | tf_op jit(solution)/shard_map/convert_element_type | solution.py:136
  187.5 8.8 %convolution_convert_fusion = bf16[2176,1024]{1,0:T(8,128)(2,1)} fusion(bf16[1024,2176]{1,0:T(8,128)(2,1)} %bitcast.66, bf16[1024,1024]{1,0:T(8,128)(2,1)S(1)} %bitcast.60), kind=kOutput, calls=%fused_computation.5 | convolution fusion | flops 4565630976 | bytes 11010048 | tf_op jit(solution)/shard_map/dot_general | solution.py:141
  197.1 42.9 %all-reduce.3.cloned.1.call-done = bf16[1024,256]{1,0:T(8,128)(2,1)} async-done(((bf16[1024,256]{1,0:T(8,128)(2,1)}), bf16[1024,256]{1,0:T(8,128)(2,1)}) %all-reduce.3.cloned.1.call-update) | async-done | bytes 524304 | tf_op jit(solution)/shard_map/psum | solution.py:130
  240.0 54.2 %reduce-scatter.2.cloned.1.call-done = bf16[272,1024]{1,0:T(8,128)(2,1)} async-done(((bf16[2176,1024]{1,0:T(8,128)(2,1)}), bf16[272,1024]{1,0:T(8,128)(2,1)}) %reduce-scatter.2.cloned.1.call-update) | async-done | bytes 557072 | tf_op jit(solution)/shard_map/reduce_scatter | solution.py:140
  294.2 1.9 copy.74
  (57 shorter events, 11.9 us)
Async XLA Ops:
  7.2 159.2 %copy-start = (bf16[1024,256]{1,0:T(8,128)(2,1)S(1)}, bf16[1024,256]{1,0:T(8,128)(2,1)}, u32[]{:S(2)}) copy-start(bf16[1024,256]{1,0:T(8,128)(2,1)} %param.18) | copy-start | bytes 1572868
  7.2 111.6 %all-gather.5.cloned.1.call-start = ((), (), s32[]{:S(2)}) async-start(), calls=%async_computation.6 | async-start | bytes 5013504 | tf_op jit(solution)/shard_map/all_gather | solution.py:25
  10.6 18.8 %all-to-all-start.2 = ((bf16[2,128,16,128]{1,3,0,2:T(8,128)(2,1)}), bf16[2,128,16,128]{1,3,0,2:T(8,128)(2,1)S(1)}, u32[]{:S(2)}, u32[]{:S(2)}) async-start(bf16[2,128,16,128]{1,3,0,2:T(8,128)(2,1)} %copy.60), calls=%async_computation.2 | async-start | bytes 2097152 | tf_op jit(solution)/shard_map/all_to_all | solution.py:37
  18.5 32.0 %copy-start.5 = (s32[2]{0:T(128)S(1)}, s32[2]{0:T(128)}, u32[]{:S(2)}) copy-start(s32[2]{0:T(128)} %param.15) | copy-start | bytes 28
  29.4 16.8 %all-to-all-start = ((bf16[2,128,16,128]{1,3,0,2:T(8,128)(2,1)}), bf16[2,128,16,128]{1,3,0,2:T(8,128)(2,1)S(1)}, u32[]{:S(2)}, u32[]{:S(2)}) async-start(bf16[2,128,16,128]{1,3,0,2:T(8,128)(2,1)} %copy.52), calls=%async_computation | async-start | bytes 2097152 | tf_op jit(solution)/shard_map/all_to_all | solution.py:35
  46.2 17.6 %all-to-all-start.1 = ((bf16[2,128,16,128]{1,3,0,2:T(8,128)(2,1)}), bf16[2,128,16,128]{1,3,0,2:T(8,128)(2,1)}, u32[]{:S(2)}, u32[]{:S(2)}) async-start(bf16[2,128,16,128]{1,3,0,2:T(8,128)(2,1)} %copy.56), calls=%async_computation.1 | async-start | bytes 2097152 | tf_op jit(solution)/shard_map/all_to_all | solution.py:36
  50.4 105.8 %all-gather.3.cloned.1.call-start = ((), (), s32[]{:S(2)}) async-start(), calls=%async_computation.5 | async-start | bytes 5570560 | tf_op jit(solution)/shard_map/all_gather | solution.py:83
  65.4 6.9 %copy-start.1 = (bf16[2,4,128,4,128]{4,2,1,3,0:T(8,128)(2,1)S(1)}, bf16[2,4,128,4,128]{4,2,1,3,0:T(8,128)(2,1)}, u32[]{:S(2)}) copy-start(bf16[2,4,128,4,128]{4,2,1,3,0:T(8,128)(2,1)} %copy.62) | copy-start | bytes 3145732
  94.3 7.3 %copy-start.4 = (f32[2]{0:T(128)S(1)}, f32[2]{0:T(128)}, u32[]{:S(2)}) copy-start(f32[2]{0:T(128)} %param.23) | copy-start | bytes 28
  94.3 7.4 %copy-start.6 = (s32[2,7]{1,0:T(2,128)S(1)}, s32[2,7]{1,0:T(2,128)}, u32[]{:S(2)}) copy-start(s32[2,7]{1,0:T(2,128)} %param.21) | copy-start | bytes 172
  94.3 8.0 %copy-start.3 = (s32[2]{0:T(128)S(1)}, s32[2]{0:T(128)}, u32[]{:S(2)}) copy-start(s32[2]{0:T(128)} %param.22) | copy-start | bytes 28
  94.4 23.2 %copy-start.7 = (s32[2,7]{1,0:T(2,128)S(1)}, s32[2,7]{1,0:T(2,128)}, u32[]{:S(2)}) copy-start(s32[2,7]{1,0:T(2,128)} %param.20) | copy-start | bytes 172
  101.6 138.4 %all-reduce.3.cloned.1.call-start = ((), (), s32[]{:S(2)}) async-start(), calls=%async_computation.8 | async-start | bytes 1048576 | tf_op jit(solution)/shard_map/psum | solution.py:130
  156.3 10.0 %copy-start.2 = (f32[7,1024]{1,0:T(8,128)S(1)}, f32[7,1024]{1,0:T(8,128)}, u32[]{:S(2)}) copy-start(f32[7,1024]{1,0:T(8,128)} %param.19) | copy-start | bytes 86020
  183.4 110.8 %reduce-scatter.2.cloned.1.call-start = ((), (), s32[]{:S(2)}) async-start(), calls=%async_computation.7 | async-start | bytes 5013504 | tf_op jit(solution)/shard_map/reduce_scatter | solution.py:140
Sparse Core Ops, SparseCore 0:
  9.6 51.7 all-gather.4
  101.7 54.4 all-gather.2
  183.5 56.4 all-reduce.2
  242.7 51.4 reduce-scatter.1
